TPU v7x, 32 devices: a whole 2x2x4 slice. The times are simulated.
32 devices in a mesh: rows: 8 (over z, y), rep: 4 (over x, core).
Axes of the slice: x: 2, y: 2, z: 4, core: 2. Of those that a mesh axis runs over, the one named last changes fastest.
Arguments:
- embed: bfloat16 [4096, 1024], P('rows'), may hold values from -6 to 6
- start: bfloat16 [4096, 128], P('rows'), may hold values from -6 to 6
- links: int32 [8, 8], P('rows'), may hold values from -1 to 3, as said below
Outputs:
- embedding: float32 [4096, 128], P('rows')
Inputs may be any that keep to these rules, and one draw needn't show every extreme that they name: `links`: entry [r, s] is -1 (no pair) or a block of owner s; the diagonal is -1; each row has at most 6 entries other than -1, and some row has exactly 6.
All inputs are finite; a program needn't handle non-finite values.
Results may differ from a plain program's by a relative error of at most 0.012.
Values may be sent and summed in bfloat16 or wider, within the bound.
A program may use at most 128 MiB of HBM per device.

v0:
```python
import math

import jax
import jax.numpy as jnp
from jax import lax
from jax.sharding import PartitionSpec as P

BLOCK = 128
BLOCKS_DEV = 4
ITERS = 2


EPSILON = 1e-06


def row_scale(rows):
    values = rows.astype(jnp.float32)
    return lax.rsqrt(jnp.mean(values * values, axis=-1) + EPSILON)


def orthonormal(result, gram_matrix):
    lower_factor = jnp.linalg.cholesky(gram_matrix)
    return lax.linalg.triangular_solve(
        lower_factor, result, left_side=False, lower=True, transpose_a=True
    )


def quarter_of(values, blocks, rep_count, quarter_index):
    shaped = values.reshape(
        (blocks, rep_count, values.shape[0] // (blocks * rep_count)) + values.shape[1:]
    )
    return lax.dynamic_index_in_dim(shaped, quarter_index, 1, keepdims=False)


def widen(block_part, rep_count, quarter_index):
    choose = (jnp.arange(rep_count) == quarter_index).astype(jnp.float32)
    expanded = block_part[:, None] * choose.reshape((1, rep_count) + (1,) * (block_part.ndim - 1))
    return expanded.reshape((-1,) + block_part.shape[2:])


def on_device(embed, start, links):
    rows_count = lax.axis_size("rows")
    rep_count = lax.axis_size("rep")
    quarter_index = lax.axis_index("rep")
    slab_rows, feature_count = embed.shape
    comp_count = start.shape[1]
    blocks = BLOCKS_DEV
    piece_rows = BLOCK // rep_count
    spread = 2.0 / math.sqrt(feature_count)
    highest = lax.Precision.HIGHEST
    slab_scale = row_scale(embed)
    own_quarter = quarter_of(embed, blocks, rep_count, quarter_index)
    quarter_scale = row_scale(own_quarter)
    link_row = links.reshape(rows_count)
    alive_dense = (link_row >= 0).astype(jnp.float32)
    asked_for = lax.all_to_all(
        links.reshape(rows_count, 1), "rows", split_axis=0, concat_axis=0, tiled=True
    )[:, 0]
    picked = jnp.clip(asked_for, 0, blocks - 1)
    placer = (asked_for[:, None] == jnp.arange(blocks)[None, :]).astype(jnp.float32)
    outgoing = jnp.take(own_quarter, picked, axis=0)
    pieces = lax.all_to_all(outgoing, "rows", split_axis=0, concat_axis=0, tiled=True)
    piece_scale = row_scale(pieces)
    products_in = jnp.einsum("pnd,rd->pnr", pieces, embed, preferred_element_type=jnp.float32)
    exponent = spread * products_in * piece_scale[:, :, None] * slab_scale[None, None, :]
    pair_tiles = (jnp.exp(exponent) * alive_dense[:, None, None]).astype(jnp.bfloat16)
    diag_products = jnp.einsum(
        "bnd,rd->bnr", own_quarter, embed, preferred_element_type=jnp.float32
    )
    diag_exponent = spread * diag_products * quarter_scale[:, :, None] * slab_scale[None, None, :]
    row_ids = (
        jnp.arange(blocks)[:, None] * BLOCK
        + quarter_index * piece_rows
        + jnp.arange(piece_rows)[None, :]
    )
    self_mask = row_ids[:, :, None] == jnp.arange(slab_rows)[None, None, :]
    diag_tile = (
        jnp.where(self_mask, 0.0, jnp.exp(diag_exponent))
        .astype(jnp.bfloat16)
        .reshape(blocks * piece_rows, slab_rows)
    )
    own_sums = jnp.sum(pair_tiles, axis=(0, 1), dtype=jnp.float32) + jnp.sum(
        diag_tile, axis=0, dtype=jnp.float32
    )
    back_sums = jnp.sum(pair_tiles, axis=2, dtype=jnp.float32)
    got_sums = lax.all_to_all(back_sums, "rows", split_axis=0, concat_axis=0, tiled=True)
    placed_sums = jnp.dot(placer.T, got_sums, precision=highest)
    degree = lax.psum(own_sums + widen(placed_sums, rep_count, quarter_index), "rep")
    inv_root = lax.rsqrt(degree)
    current = start.astype(jnp.float32)
    scaled = (current * inv_root[:, None]).astype(jnp.bfloat16)
    for turn_index in range(ITERS):
        scaled_quarter = quarter_of(scaled, blocks, rep_count, quarter_index)
        outgoing_iterate = jnp.take(scaled_quarter, picked, axis=0)
        reverse = jnp.einsum("pnr,rk->pnk", pair_tiles, scaled, preferred_element_type=jnp.float32)
        returned = lax.all_to_all(reverse, "rows", split_axis=0, concat_axis=0, tiled=True)
        fetched = lax.all_to_all(outgoing_iterate, "rows", split_axis=0, concat_axis=0, tiled=True)
        forward = lax.dot_general(
            pair_tiles, fetched, (((0, 1), (0, 1)), ((), ())), preferred_element_type=jnp.float32
        )
        forward = forward + lax.dot_general(
            diag_tile,
            scaled_quarter.reshape(blocks * piece_rows, comp_count),
            (((0,), (0,)), ((), ())),
            preferred_element_type=jnp.float32,
        )
        placed = jnp.einsum("pb,pnk->bnk", placer, returned, precision=highest)
        summed_part = forward + widen(placed, rep_count, quarter_index)
        summed_all = lax.psum(summed_part, "rep")
        result = summed_all * inv_root[:, None]
        gram_matrix = lax.psum(jnp.dot(result.T, result, precision=highest), "rows")
        current = orthonormal(result, gram_matrix)
        scaled = (current * inv_root[:, None]).astype(jnp.bfloat16)
    return current * math.sqrt(slab_rows * rows_count)


def solution(mesh):
    return jax.shard_map(
        on_device,
        mesh=mesh,
        in_specs=(P("rows", None), P("rows", None), P("rows", None)),
        out_specs=P("rows", None),
        check_vma=False,
    )
```

profile of v0, /device:TPU:0, one launch (start us, length us, event | category | flops | bytes accessed | tf_op | source)
XLA Modules:
  0.0 369.6 jit_solution(8929522240494461467)
XLA Ops:
  6.5 1.4 copy.25
  7.9 7.3 %all-to-all-start = ((s32[8,1,1]{2,1,0:T(1,128)}), s32[8,1,1]{2,1,0:T(1,128)S(1)}, u32[]{:S(2)}, u32[]{:S(2)}) async-start(s32[8,1,1]{2,1,0:T(1,128)} %copy.25), calls=%async_computation | async-start | bytes 8192 | tf_op jit(solution)/shard_map/all_to_all | solution.py:56
  15.3 1.5 multiply_reduce_fusion
  16.9 0.1 multiply_reduce_fusion.2
  17.1 0.1 mul.174
  17.2 4.5 %all-to-all-done = s32[8,1,1]{2,1,0:T(1,128)S(1)} async-done(((s32[8,1,1]{2,1,0:T(1,128)}), s32[8,1,1]{2,1,0:T(1,128)S(1)}, u32[]{:S(2)}, u32[]{:S(2)}) %all-to-all-start) | async-done | bytes 64 | tf_op jit(solution)/shard_map/all_to_all | solution.py:56
  21.7 0.4 fusion.50
  22.1 0.6 gather_fusion
  22.7 0.9 broadcast_select_fusion
  23.6 3.5 all-to-all-start.1
  27.1 0.5 convert_reduce_fusion.2
  27.7 12.7 %all-to-all-done.1 = bf16[8,32,1024]{2,1,0:T(8,128)(2,1)S(1)} async-done(((bf16[8,32,1024]{2,1,0:T(8,128)(2,1)}), bf16[8,32,1024]{2,1,0:T(8,128)(2,1)S(1)}, u32[]{:S(2)}, u32[]{:S(2)}) %all-to-all-start.1) | async-done | bytes 524320 | tf_op jit(solution)/shard_map/all_to_all | solution.py:62
  40.4 0.2 multiply_reduce_fusion.1
  40.6 1.2 convert_reduce_fusion.1
  41.8 3.7 all-to-all-start.2
  45.4 6.4 %all-to-all-done.2 = f32[8,1,32]{2,1,0:T(1,128)S(1)} async-done(((f32[8,1,32]{2,1,0:T(1,128)}), f32[8,1,32]{2,1,0:T(1,128)S(1)}, u32[]{:S(2)}, u32[]{:S(2)}) %all-to-all-start.2) | async-done | bytes 1056 | tf_op jit(solution)/shard_map/all_to_all | solution.py:86
  51.9 0.1 fusion.42
  52.0 0.1 mul.172
  52.1 5.7 %psum.35 = f32[512]{0:T(512)S(1)} all-reduce(f32[512]{0:T(512)S(1)} %multiply_add_fusion), channel_id=1, replica_groups=mesh['rows'=8,'rep'=4] {'rep'}, use_global_device_ids=true, to_apply=%region_6.7 | all-reduce | flops 512 | bytes 4096 | tf_op jit(solution)/shard_map/psum | solution.py:88
  57.7 0.1 multiply_convert_fusion
  57.9 0.6 gather_fusion.1
  58.5 0.7 broadcast_select_fusion.1
  59.2 3.3 all-to-all-start.3
  62.5 0.9 fusion.23
  63.4 6.0 %all-to-all-done.3 = bf16[8,32,128]{2,1,0:T(8,128)(2,1)S(1)} async-done(((bf16[8,32,128]{2,1,0:T(8,128)(2,1)}), bf16[8,32,128]{2,1,0:T(8,128)(2,1)S(1)}, u32[]{:S(2)}, u32[]{:S(2)}) %all-to-all-start.3) | async-done | bytes 65568 | tf_op jit(solution)/shard_map/all_to_all | solution.py:97
  69.4 3.4 all-to-all-start.4
  72.8 0.3 convolution_bitcast_fusion.3
  73.1 6.9 %all-to-all-done.4 = f32[8,32,128]{2,1,0:T(8,128)S(1)} async-done(((f32[8,32,128]{2,1,0:T(8,128)}), f32[8,32,128]{2,1,0:T(8,128)S(1)}, u32[]{:S(2)}, u32[]{:S(2)}) %all-to-all-start.4) | async-done | bytes 131104 | tf_op jit(solution)/shard_map/all_to_all | solution.py:96
  80.0 0.3 fusion.27
  80.3 0.1 bitcast_multiply_fusion.1
  80.4 0.9 fusion.5
  81.4 30.4 %all-reduce.5.cloned.1.call-done = f32[512,128]{1,0:T(8,128)} async-done(((f32[512,128]{1,0:T(8,128)}), f32[512,128]{1,0:T(8,128)}) %all-reduce.5.cloned.1.call-update) | async-done | bytes 262160 | tf_op jit(solution)/shard_map/psum | solution.py:109
  111.8 2.5 fusion.19
  114.3 70.2 %all-reduce.7.cloned.1.call-done = f32[128,128]{0,1:T(8,128)} async-done(((f32[128,128]{0,1:T(8,128)}), f32[128,128]{0,1:T(8,128)}) %all-reduce.7.cloned.1.call-update) | async-done | bytes 65552 | tf_op jit(solution)/shard_map/psum | solution.py:111
  184.5 0.9 copy.30
  185.4 0.9 fusion.38
  186.3 11.7 %cholesky.44 = f32[128,128]{1,0:T(8,128)S(1)} custom-call(f32[128,128]{1,0:T(8,128)S(1)} %fusion.38), custom_call_target="Cholesky" | custom-call | tf_op jit(solution)/shard_map/jit(cholesky)/cholesky | solution.py:22
  198.0 0.6 compare_reduce_fusion.1
  198.7 0.7 fusion.33
  199.3 9.8 %custom-call.6 = f32[1,128,128]{1,2,0:T(8,128)S(1)} custom-call(f32[1,128,128]{2,1,0:T(8,128)S(1)} %fusion.33), custom_call_target="InvertDiagBlocksLowerTriangular" | custom-call | tf_op jit(solution)/shard_map/triangular_solve/custom-call.0 | solution.py:23
  209.2 0.4 fusion.11
  209.6 0.6 gather_fusion.2
  210.2 0.7 broadcast_select_fusion.2
  210.9 4.5 %all-to-all-start.5 = ((bf16[8,32,128]{2,1,0:T(8,128)(2,1)}), bf16[8,32,128]{2,1,0:T(8,128)(2,1)S(1)}, u32[]{:S(2)}, u32[]{:S(2)}) async-start(bf16[8,32,128]{2,1,0:T(8,128)(2,1)} %broadcast_select_fusion.2), calls=%async_computation.5 | async-start | bytes 131072 | tf_op jit(solution)/shard_map/all_to_all | solution.py:97
  215.4 0.9 fusion.21
  216.3 6.0 %all-to-all-done.5 = bf16[8,32,128]{2,1,0:T(8,128)(2,1)S(1)} async-done(((bf16[8,32,128]{2,1,0:T(8,128)(2,1)}), bf16[8,32,128]{2,1,0:T(8,128)(2,1)S(1)}, u32[]{:S(2)}, u32[]{:S(2)}) %all-to-all-start.5) | async-done | bytes 65568 | tf_op jit(solution)/shard_map/all_to_all | solution.py:97
  222.3 3.4 all-to-all-start.6
  225.7 0.2 all-reduce.9.cloned.1.call-start
  225.9 0.3 convolution_bitcast_fusion.1
  226.2 6.8 %all-to-all-done.6 = f32[8,32,128]{2,1,0:T(8,128)S(1)} async-done(((f32[8,32,128]{2,1,0:T(8,128)}), f32[8,32,128]{2,1,0:T(8,128)S(1)}, u32[]{:S(2)}, u32[]{:S(2)}) %all-to-all-start.6) | async-done | bytes 131104 | tf_op jit(solution)/shard_map/all_to_all | solution.py:96
  233.0 0.3 fusion.25
  233.3 0.1 bitcast_multiply_fusion
  233.4 0.9 fusion.4
  234.4 30.1 %all-reduce.9.cloned.1.call-done = f32[512,128]{1,0:T(8,128)} async-done(((f32[512,128]{1,0:T(8,128)}), f32[512,128]{1,0:T(8,128)}) %all-reduce.9.cloned.1.call-update) | async-done | bytes 262160 | tf_op jit(solution)/shard_map/psum | solution.py:109
  264.5 2.5 fusion.16
  267.0 70.0 %all-reduce.11.cloned.1.call-done = f32[128,128]{0,1:T(8,128)} async-done(((f32[128,128]{0,1:T(8,128)}), f32[128,128]{0,1:T(8,128)}) %all-reduce.11.cloned.1.call-update) | async-done | bytes 65552 | tf_op jit(solution)/shard_map/psum | solution.py:111
  337.0 0.9 copy.35
  338.0 0.9 fusion.36
  338.8 11.7 %cholesky.55 = f32[128,128]{1,0:T(8,128)S(1)} custom-call(f32[128,128]{1,0:T(8,128)S(1)} %fusion.36), custom_call_target="Cholesky" | custom-call | tf_op jit(solution)/shard_map/jit(cholesky)/cholesky | solution.py:22
  350.6 0.6 compare_reduce_fusion
  351.2 0.7 fusion.34
  351.9 9.8 %custom-call.7 = f32[1,128,128]{1,2,0:T(8,128)S(1)} custom-call(f32[1,128,128]{2,1,0:T(8,128)S(1)} %fusion.34), custom_call_target="InvertDiagBlocksLowerTriangular" | custom-call | tf_op jit(solution)/shard_map/triangular_solve/custom-call.0 | solution.py:23
  361.7 0.5 fusion.6
  362.2 0.8 copy.36
  (40 shorter events, 0.6 us)
Async XLA Ops:
  6.5 10.3 %copy-start = (bf16[512,1024]{1,0:T(8,128)(2,1)S(1)}, bf16[512,1024]{1,0:T(8,128)(2,1)}, u32[]{:S(2)}) copy-start(bf16[512,1024]{1,0:T(8,128)(2,1)} %param.8) | copy-start | bytes 3145732
  7.9 13.7 %all-to-all-start = ((s32[8,1,1]{2,1,0:T(1,128)}), s32[8,1,1]{2,1,0:T(1,128)S(1)}, u32[]{:S(2)}, u32[]{:S(2)}) async-start(s32[8,1,1]{2,1,0:T(1,128)} %copy.25), calls=%async_computation | async-start | bytes 8192 | tf_op jit(solution)/shard_map/all_to_all | solution.py:56
  22.7 4.4 %copy-start.4 = (s32[1,8]{1,0:T(1,128)S(1)}, s32[1,8]{1,0:T(1,128)}, u32[]{:S(2)}) copy-start(s32[1,8]{1,0:T(1,128)} %param.10) | copy-start | bytes 100
  23.6 16.8 %all-to-all-start.1 = ((bf16[8,32,1024]{2,1,0:T(8,128)(2,1)}), bf16[8,32,1024]{2,1,0:T(8,128)(2,1)S(1)}, u32[]{:S(2)}, u32[]{:S(2)}) async-start(bf16[8,32,1024]{2,1,0:T(8,128)(2,1)} %broadcast_select_fusion), calls=%async_computation.1 | async-start | bytes 1048576 | tf_op jit(solution)/shard_map/all_to_all | solution.py:62
  40.5 17.2 %copy-start.3 = (bf16[512,128]{1,0:T(8,128)(2,1)S(1)}, bf16[512,128]{1,0:T(8,128)(2,1)}, u32[]{:S(2)}) copy-start(bf16[512,128]{1,0:T(8,128)(2,1)} %param.9) | copy-start | bytes 393220
  41.8 10.1 %all-to-all-start.2 = ((f32[8,1,32]{2,1,0:T(1,128)}), f32[8,1,32]{2,1,0:T(1,128)S(1)}, u32[]{:S(2)}, u32[]{:S(2)}) async-start(f32[8,1,32]{2,1,0:T(1,128)} %bitcast.6), calls=%async_computation.2 | async-start | bytes 8192 | tf_op jit(solution)/shard_map/all_to_all | solution.py:86
  59.2 10.2 %all-to-all-start.3 = ((bf16[8,32,128]{2,1,0:T(8,128)(2,1)}), bf16[8,32,128]{2,1,0:T(8,128)(2,1)S(1)}, u32[]{:S(2)}, u32[]{:S(2)}) async-start(bf16[8,32,128]{2,1,0:T(8,128)(2,1)} %broadcast_select_fusion.1), calls=%async_computation.3 | async-start | bytes 131072 | tf_op jit(solution)/shard_map/all_to_all | solution.py:97
  69.4 10.7 %all-to-all-start.4 = ((f32[8,32,128]{2,1,0:T(8,128)}), f32[8,32,128]{2,1,0:T(8,128)S(1)}, u32[]{:S(2)}, u32[]{:S(2)}) async-start(f32[8,32,128]{2,1,0:T(8,128)} %fusion.23), calls=%async_computation.4 | async-start | bytes 262144 | tf_op jit(solution)/shard_map/all_to_all | solution.py:96
  72.7 39.1 %all-reduce.5.cloned.1.call-start = ((), (), s32[]{:S(2)}) async-start(), calls=%async_computation.7 | async-start | bytes 524288 | tf_op jit(solution)/shard_map/psum | solution.py:109
  81.4 103.1 %all-reduce.7.cloned.1.call-start = ((), (), s32[]{:S(2)}) async-start(), calls=%async_computation.8 | async-start | bytes 131072 | tf_op jit(solution)/shard_map/psum | solution.py:111
  111.8 97.3 %copy-start.1 = (f32[512,128]{1,0:T(8,128)S(1)}, f32[512,128]{1,0:T(8,128)}, u32[]{:S(2)}) copy-start(f32[512,128]{1,0:T(8,128)} %all-reduce.5.cloned.1.call-done) | copy-start | bytes 786436
  210.9 11.4 %all-to-all-start.5 = ((bf16[8,32,128]{2,1,0:T(8,128)(2,1)}), bf16[8,32,128]{2,1,0:T(8,128)(2,1)S(1)}, u32[]{:S(2)}, u32[]{:S(2)}) async-start(bf16[8,32,128]{2,1,0:T(8,128)(2,1)} %broadcast_select_fusion.2), calls=%async_computation.5 | async-start | bytes 131072 | tf_op jit(solution)/shard_map/all_to_all | solution.py:97
  222.3 10.7 %all-to-all-start.6 = ((f32[8,32,128]{2,1,0:T(8,128)}), f32[8,32,128]{2,1,0:T(8,128)S(1)}, u32[]{:S(2)}, u32[]{:S(2)}) async-start(f32[8,32,128]{2,1,0:T(8,128)} %fusion.21), calls=%async_computation.6 | async-start | bytes 262144 | tf_op jit(solution)/shard_map/all_to_all | solution.py:96
  225.7 38.8 %all-reduce.9.cloned.1.call-start = ((), (), s32[]{:S(2)}) async-start(), calls=%async_computation.9 | async-start | bytes 524288 | tf_op jit(solution)/shard_map/psum | solution.py:109
  234.3 102.7 %all-reduce.11.cloned.1.call-start = ((), (), s32[]{:S(2)}) async-start(), calls=%async_computation.10 | async-start | bytes 131072 | tf_op jit(solution)/shard_map/psum | solution.py:111
  264.5 97.2 %copy-start.2 = (f32[512,128]{1,0:T(8,128)S(1)}, f32[512,128]{1,0:T(8,128)}, u32[]{:S(2)}) copy-start(f32[512,128]{1,0:T(8,128)} %all-reduce.9.cloned.1.call-done) | copy-start | bytes 786436
Sparse Core Ops, SparseCore 0:
  81.5 30.2 all-reduce.4
  115.2 69.2 all-reduce.6
  234.5 29.9 all-reduce.8
  267.8 69.2 all-reduce.10
where the time goes:
time: 371 us; the launch traced here: 370 us
  waiting for transfers between devices  250 us (67%)
  other arithmetic  52.4 us (14%)
  starting transfers between devices  29.4 us (8%)
  between operations  13.5 us (4%)
  matrix products  12.4 us (3%)
  local copies, waits for them, and re-layouts  6.14 us (2%)
  blocking collectives  5.65 us (2%)
    psum x2, waiting for transfers between devices, on_device(): gram_matrix = lax.psum(jnp.dot(result.T, result, precision=highest), 'rows')  140 us
    psum x2, waiting for transfers between devices, on_device(): summed_all = lax.psum(summed_part, 'rep')  60.5 us
    another operation x6, other arithmetic, orthonormal(): lower_factor = jnp.linalg.cholesky(gram_matrix)  24.8 us
    another operation x4, other arithmetic, orthonormal(): lax.linalg.triangular_solve(lower_factor, result, left_side=False, lower=...  20.9 us
    all_to_all x2, waiting for transfers between devices, on_device(): lax.all_to_all(reverse, 'rows', split_axis=0, concat_axis=0, tiled=True)  13.7 us
    all_to_all x1, waiting for transfers between devices, on_device(): lax.all_to_all(outgoing, 'rows', split_axis=0, concat_axis=0, tiled=True)  12.7 us
    all_to_all x2, waiting for transfers between devices, on_device(): lax.all_to_all(outgoing_iterate, 'rows', split_axis=0, concat_axis=0, til...  12 us
    all_to_all x2, starting transfers between devices, on_device(): lax.all_to_all(outgoing_iterate, 'rows', split_axis=0, concat_axis=0, til...  7.89 us
  transfers between devices with their start and end apart: 11, of which 11 were waited for; matrix products, arithmetic and copies ran while one was open for 1% of the time, Pallas kernels for 0%

commit v1 on v0

v1 whole, which is shorter than its diff:
```python
import functools
import math

import jax
import jax.numpy as jnp
from jax import lax
from jax.experimental import pallas as pl
from jax.experimental.pallas import tpu as pltpu
from jax.sharding import PartitionSpec as P

BLOCK = 128
BLOCKS_DEV = 4
ITERS = 2
LANES = 128
EPSILON = 1e-06
HIGHEST = lax.Precision.HIGHEST
F32 = jnp.float32
BF16 = jnp.bfloat16


def dot(a, b, dims, precision=None):
    return lax.dot_general(
        a, b, (dims, ((), ())), precision=precision, preferred_element_type=F32
    )


def inv_rms(rows):
    values = rows.astype(F32)
    return lax.rsqrt(jnp.mean(values * values, axis=1, keepdims=True) + EPSILON)


def as_row(column):
    return jnp.broadcast_to(column, (column.shape[0], LANES)).T[0:1, :]


def kernel(
    n, reps,
    embed, start, links, out,
    link_in, asked, alive, own, picks, pieces, tiles, tiles_t, square,
    u_full, u_out, u_in, rev_out, rev_in, part_out, part_in, y_own, y_in, inv, placed,
    g_out, g_in, slice_out, slice_in, total_out, gram, elim,
    link_send, link_recv, embed_send, embed_recv, u_send, u_recv, rev_send, rev_recv,
    part_send, part_recv, y_send, y_recv, g_send, g_recv, slice_send, slice_recv,
    total_send, total_recv,
):
    me = lax.axis_index("rows")
    quarter = lax.axis_index("rep")
    slab, features = embed.shape
    comps = start.shape[1]
    blocks = BLOCKS_DEV
    piece = BLOCK // reps
    own_rows = blocks * piece
    spread = 2.0 / math.sqrt(features)
    group = min(n, 8)
    chunk = group * piece
    unroll = n <= 8

    def over(count, body, low=0):
        if unroll:
            for index in range(low, count):
                body(index)
        else:
            def step(index, carry):
                body(index)
                return carry
            lax.fori_loop(low, count, step, 0)

    def peer(distance):
        return lax.rem(me + distance, n)

    def rep_peer(distance):
        return lax.rem(quarter + distance, reps)

    def to_rows(src, dst, send, recv, target):
        return pltpu.make_async_remote_copy(
            src_ref=src, dst_ref=dst, send_sem=send, recv_sem=recv,
            device_id={"rows": target}, device_id_type=pl.DeviceIdType.MESH,
        )

    def to_rep(src, dst, send, recv, target):
        return pltpu.make_async_remote_copy(
            src_ref=src, dst_ref=dst, send_sem=send, recv_sem=recv,
            device_id={"rep": target}, device_id_type=pl.DeviceIdType.MESH,
        )

    def own_at(block, which):
        return pl.ds(pl.multiple_of(block * BLOCK + which * piece, piece), piece)

    barrier = pltpu.get_barrier_semaphore()

    def greet(distance):
        pl.semaphore_signal(
            barrier, inc=1, device_id={"rows": peer(distance)},
            device_id_type=pl.DeviceIdType.MESH,
        )

    over(n, greet, 1)
    for distance in range(1, reps):
        pl.semaphore_signal(
            barrier, inc=1, device_id={"rep": rep_peer(distance)},
            device_id_type=pl.DeviceIdType.MESH,
        )
    pl.semaphore_wait(barrier, n + reps - 2)

    def link_copy(s):
        return to_rows(links, link_in.at[me], link_send.at[s], link_recv.at[me], s)

    def link_got(s):
        return to_rows(links, link_in.at[s], link_send.at[s], link_recv.at[s], s)

    over(n, lambda d: link_copy(peer(d)).start(), 1)
    lane = lax.broadcasted_iota(jnp.int32, (8, LANES), 1)
    link_in[me] = links[...]
    pieces[me] = jnp.zeros((piece, features), BF16)

    for b in range(blocks):
        own[b] = embed[own_at(b, quarter), :]
    own_flat = own[...].reshape(own_rows, features)
    own_scale = inv_rms(own_flat)
    slab_scale = jnp.concatenate(
        [inv_rms(embed[b * BLOCK:(b + 1) * BLOCK, :]) for b in range(blocks)], axis=0
    )
    scale_row = as_row(slab_scale)

    def alive_of(s):
        entry = jnp.sum(jnp.where(lane == s, links[...], 0).astype(F32), axis=1, keepdims=True)
        alive[s] = jnp.broadcast_to(
            jnp.where(entry[0:1] >= 0.0, 1.0, 0.0), (piece, LANES)
        )

    over(n, alive_of)

    def pick(d):
        s = peer(d)
        link_got(s).wait_recv()
        entry = jnp.sum(
            jnp.where(lane == me, link_in[s], 0).astype(F32), axis=1, keepdims=True
        )
        asked[s] = jnp.broadcast_to(entry, (8, LANES))
        chosen = jnp.maximum(entry[0:1], 0.0)
        mixed = jnp.zeros((piece, features), F32)
        for b in range(blocks):
            mixed = mixed + jnp.where(chosen == float(b), 1.0, 0.0) * own[b].astype(F32)
        picks[s] = mixed.astype(BF16)
        to_rows(picks.at[s], pieces.at[me], embed_send.at[s], embed_recv.at[me], s).start()

    over(n, pick, 1)

    products = dot(embed[...], own_flat, ((1,), (1,)))
    affinity = jnp.exp(spread * products * slab_scale * as_row(own_scale))
    row_id = lax.broadcasted_iota(jnp.int32, (slab, own_rows), 0)
    col_id = lax.broadcasted_iota(jnp.int32, (slab, own_rows), 1)
    col_row = (col_id // piece) * BLOCK + quarter * piece + col_id % piece
    square[...] = jnp.where(row_id == col_row, 0.0, affinity).astype(BF16)

    def embed_got(d):
        s = peer(d)
        to_rows(picks.at[s], pieces.at[s], embed_send.at[s], embed_recv.at[s], s).wait_recv()

    over(n, embed_got, 1)

    def tile_chunk(index):
        first = index * group
        rows = pieces[pl.ds(first, group)].reshape(chunk, features)
        live = alive[pl.ds(first, group)].reshape(chunk, LANES)[:, 0:1]
        values = dot(rows, embed[...], ((1,), (1,)))
        values = jnp.exp(spread * values * inv_rms(rows) * scale_row) * live
        values = values.astype(BF16)
        tiles[index] = values
        tiles_t[index] = values.astype(F32).T.astype(BF16)

    over(n // group, tile_chunk)

    def product(phase, u_turn):
        if u_turn is not None:
            for b in range(blocks):
                own_u = u_full[own_at(b, quarter), :]
                u_own_parts.append(own_u)
            own_us = u_own_parts[-blocks:]

            def send_u(d):
                s = peer(d)
                chosen = jnp.maximum(asked[s][0:1, :], 0.0)
                mixed = jnp.zeros((piece, comps), F32)
                for b in range(blocks):
                    mixed = mixed + jnp.where(chosen == float(b), 1.0, 0.0) * own_us[b].astype(F32)
                u_out[u_turn, s] = mixed.astype(BF16)
                to_rows(
                    u_out.at[u_turn, s], u_in.at[u_turn, me],
                    u_send.at[u_turn, s], u_recv.at[u_turn, me], s,
                ).start()

            over(n, send_u, 1)
            u_in[u_turn, me] = jnp.zeros((piece, comps), BF16)

        def reverse(index):
            result = dot(tiles[index], u_full[...], ((1,), (0,)))
            rev_out[phase, pl.ds(index * group, group)] = result.reshape(group, piece, comps)

        over(n // group, reverse)

        def send_rev(d):
            s = peer(d)
            to_rows(
                rev_out.at[phase, s], rev_in.at[phase, me],
                rev_send.at[phase, s], rev_recv.at[phase, me], s,
            ).start()

        over(n, send_rev, 1)
        if u_turn is None:
            u_mine = jnp.ones((own_rows, comps), BF16)
        else:
            u_mine = jnp.concatenate(own_us, axis=0)
        forward = dot(square[...], u_mine, ((1,), (0,)))
        if u_turn is not None:
            def u_got(d):
                s = peer(d)
                to_rows(
                    u_out.at[u_turn, s], u_in.at[u_turn, s],
                    u_send.at[u_turn, s], u_recv.at[u_turn, s], s,
                ).wait_recv()

            over(n, u_got, 1)

        def forward_chunk(index, sofar):
            if u_turn is None:
                fetched = jnp.ones((chunk, comps), BF16)
            else:
                fetched = u_in[u_turn, pl.ds(index * group, group)].reshape(chunk, comps)
            return sofar + dot(tiles_t[index], fetched, ((1,), (0,)))

        if n // group == 1:
            forward = forward_chunk(0, forward)
        else:
            forward = lax.fori_loop(0, n // group, forward_chunk, forward)
        for t in range(reps):
            for b in range(blocks):
                low = b * BLOCK + t * piece
                part_out[phase, t, b * piece:(b + 1) * piece] = forward[low:low + piece]
        for d in range(1, reps):
            t = rep_peer(d)
            to_rep(
                part_out.at[phase, t], part_in.at[phase, quarter],
                part_send.at[phase, t], part_recv.at[phase, quarter], t,
            ).start()
        placed[...] = part_out[phase, quarter]

        def place(d):
            s = peer(d)
            to_rows(
                rev_out.at[phase, s], rev_in.at[phase, s],
                rev_send.at[phase, s], rev_recv.at[phase, s], s,
            ).wait_recv()
            chosen = asked[s][0:1, :]
            value = rev_in[phase, s]
            for b in range(blocks):
                at = pl.ds(b * piece, piece)
                placed[at, :] = placed[at, :] + jnp.where(chosen == float(b), 1.0, 0.0) * value

        over(n, place, 1)
        result = placed[...]
        for d in range(1, reps):
            t = rep_peer(d)
            to_rep(
                part_out.at[phase, t], part_in.at[phase, t],
                part_send.at[phase, t], part_recv.at[phase, t], t,
            ).wait_recv()
            result = result + part_in[phase, t]
        return result

    def share(phase, values):
        y_own[phase] = values
        for d in range(1, reps):
            t = rep_peer(d)
            to_rep(
                y_own.at[phase], y_in.at[phase, quarter],
                y_send.at[phase, t], y_recv.at[phase, quarter], t,
            ).start()
        y_in[phase, quarter] = values

    def shared(phase):
        for d in range(1, reps):
            t = rep_peer(d)
            to_rep(
                y_own.at[phase], y_in.at[phase, t],
                y_send.at[phase, t], y_recv.at[phase, t], t,
            ).wait_recv()

    u_own_parts = []
    u_full[...] = jnp.ones((slab, comps), BF16)
    degree = product(0, None)
    share(0, degree)
    inv_own = lax.rsqrt(degree)
    shared(0)
    for t in range(reps):
        for b in range(blocks):
            low = b * BLOCK + t * piece
            inv[low:low + piece] = lax.rsqrt(y_in[0, t, b * piece:(b + 1) * piece])
    u_full[...] = (start[...].astype(F32) * inv[...]).astype(BF16)

    part = comps // reps
    sub_c = lax.broadcasted_iota(jnp.int32, (comps, comps), 0)
    lane_c = lax.broadcasted_iota(jnp.int32, (comps, comps), 1)
    sub_1 = lax.broadcasted_iota(jnp.int32, (comps, 1), 0)
    lane_1 = lax.broadcasted_iota(jnp.int32, (1, comps), 1)

    for turn in range(ITERS):
        phase = turn + 1
        y_mine = product(phase, turn) * inv_own
        partial = dot(y_mine.T, y_mine, ((1,), (0,)), HIGHEST)
        g_out[turn] = partial.reshape(reps, part, comps)
        for d in range(1, reps):
            t = rep_peer(d)
            to_rep(
                g_out.at[turn, t], g_in.at[turn, quarter],
                g_send.at[turn, t], g_recv.at[turn, quarter], t,
            ).start()
        share(phase, y_mine)
        slice_sum = g_out[turn, quarter]
        for d in range(1, reps):
            t = rep_peer(d)
            to_rep(
                g_out.at[turn, t], g_in.at[turn, t],
                g_send.at[turn, t], g_recv.at[turn, t], t,
            ).wait_recv()
            slice_sum = slice_sum + g_in[turn, t]
        slice_out[turn] = slice_sum
        slice_in[turn, me] = slice_sum

        def send_slice(d):
            s = peer(d)
            to_rows(
                slice_out.at[turn], slice_in.at[turn, me],
                slice_send.at[turn, s], slice_recv.at[turn, me], s,
            ).start()

        def slice_got(d):
            s = peer(d)
            to_rows(
                slice_out.at[turn], slice_in.at[turn, s],
                slice_send.at[turn, s], slice_recv.at[turn, s], s,
            ).wait_recv()

        over(n, send_slice, 1)
        over(n, slice_got, 1)
        slice_total = jnp.sum(slice_in[turn], axis=0)
        total_out[turn] = slice_total
        for d in range(1, reps):
            t = rep_peer(d)
            to_rep(
                total_out.at[turn], gram.at[turn, quarter],
                total_send.at[turn, t], total_recv.at[turn, quarter], t,
            ).start()
        gram[turn, quarter] = slice_total
        for d in range(1, reps):
            t = rep_peer(d)
            to_rep(
                total_out.at[turn], gram.at[turn, t],
                total_send.at[turn, t], total_recv.at[turn, t], t,
            ).wait_recv()

        elim[:, 0:comps] = gram[turn].reshape(comps, comps)
        elim[:, comps:2 * comps] = jnp.where(sub_c == lane_c, 1.0, 0.0)

        def eliminate(k, carry):
            row = elim[pl.ds(k, 1), :]
            left = elim[:, 0:comps]
            column = jnp.sum(jnp.where(lane_c == k, left, 0.0), axis=1, keepdims=True)
            pivot = jnp.sum(jnp.where(lane_1 == k, row[:, 0:comps], 0.0), axis=1, keepdims=True)
            factor = jnp.where(sub_1 > k, column / pivot, 0.0)
            elim[...] = elim[...] - factor * row
            return carry

        lax.fori_loop(0, comps, eliminate, 0)
        pivots = jnp.sum(
            jnp.where(sub_c == lane_c, elim[:, 0:comps], 0.0), axis=1, keepdims=True
        )
        lower_inv = elim[:, comps:2 * comps] * lax.rsqrt(pivots)
        shared(phase)
        last = turn == ITERS - 1
        for t in range(reps):
            fresh = dot(y_in[phase, t], lower_inv, ((1,), (1,)), HIGHEST)
            for b in range(blocks):
                low = b * BLOCK + t * piece
                rows = fresh[b * piece:(b + 1) * piece]
                if last:
                    out[low:low + piece] = rows * math.sqrt(slab * n)
                else:
                    u_full[low:low + piece] = (rows * inv[low:low + piece]).astype(BF16)

    def sent_rows(d):
        s = peer(d)
        link_copy(s).wait_send()
        to_rows(picks.at[s], pieces.at[me], embed_send.at[s], embed_recv.at[me], s).wait_send()
        for phase in range(ITERS + 1):
            to_rows(
                rev_out.at[phase, s], rev_in.at[phase, me],
                rev_send.at[phase, s], rev_recv.at[phase, me], s,
            ).wait_send()
        for turn in range(ITERS):
            to_rows(
                u_out.at[turn, s], u_in.at[turn, me],
                u_send.at[turn, s], u_recv.at[turn, me], s,
            ).wait_send()
            to_rows(
                slice_out.at[turn], slice_in.at[turn, me],
                slice_send.at[turn, s], slice_recv.at[turn, me], s,
            ).wait_send()

    over(n, sent_rows, 1)
    for d in range(1, reps):
        t = rep_peer(d)
        for phase in range(ITERS + 1):
            to_rep(
                part_out.at[phase, t], part_in.at[phase, quarter],
                part_send.at[phase, t], part_recv.at[phase, quarter], t,
            ).wait_send()
            to_rep(
                y_own.at[phase], y_in.at[phase, quarter],
                y_send.at[phase, t], y_recv.at[phase, quarter], t,
            ).wait_send()
        for turn in range(ITERS):
            to_rep(
                g_out.at[turn, t], g_in.at[turn, quarter],
                g_send.at[turn, t], g_recv.at[turn, quarter], t,
            ).wait_send()
            to_rep(
                total_out.at[turn], gram.at[turn, quarter],
                total_send.at[turn, t], total_recv.at[turn, quarter], t,
            ).wait_send()


def on_device(n, reps, embed, start, links):
    slab, features = embed.shape
    comps = start.shape[1]
    piece = BLOCK // reps
    own_rows = BLOCKS_DEV * piece
    part = comps // reps
    group = min(n, 8)
    phases = ITERS + 1
    wide = jnp.broadcast_to(
        jnp.pad(links, ((0, 0), (0, LANES - n)), constant_values=-1), (8, LANES)
    )
    vmem = pltpu.VMEM
    sem = pltpu.SemaphoreType.DMA
    scratch = [
        vmem((n, 8, LANES), jnp.int32),
        vmem((n, 8, LANES), F32),
        vmem((n, piece, LANES), F32),
        vmem((BLOCKS_DEV, piece, features), BF16),
        vmem((n, piece, features), BF16),
        vmem((n, piece, features), BF16),
        vmem((n // group, group * piece, slab), BF16),
        vmem((n // group, slab, group * piece), BF16),
        vmem((slab, own_rows), BF16),
        vmem((slab, comps), BF16),
        vmem((ITERS, n, piece, comps), BF16),
        vmem((ITERS, n, piece, comps), BF16),
        vmem((phases, n, piece, comps), F32),
        vmem((phases, n, piece, comps), F32),
        vmem((phases, reps, own_rows, comps), F32),
        vmem((phases, reps, own_rows, comps), F32),
        vmem((phases, own_rows, comps), F32),
        vmem((phases, reps, own_rows, comps), F32),
        vmem((slab, comps), F32),
        vmem((own_rows, comps), F32),
        vmem((ITERS, reps, part, comps), F32),
        vmem((ITERS, reps, part, comps), F32),
        vmem((ITERS, part, comps), F32),
        vmem((ITERS, n, part, comps), F32),
        vmem((ITERS, part, comps), F32),
        vmem((ITERS, reps, part, comps), F32),
        vmem((comps, 2 * comps), F32),
    ]
    sems = [
        (n,), (n,), (n,), (n,), (ITERS, n), (ITERS, n), (phases, n), (phases, n),
        (phases, reps), (phases, reps), (phases, reps), (phases, reps),
        (ITERS, reps), (ITERS, reps), (ITERS, n), (ITERS, n), (ITERS, reps), (ITERS, reps),
    ]
    return pl.pallas_call(
        functools.partial(kernel, n, reps),
        out_shape=jax.ShapeDtypeStruct((slab, comps), F32),
        in_specs=[pl.BlockSpec(memory_space=pltpu.VMEM)] * 3,
        out_specs=pl.BlockSpec(memory_space=pltpu.VMEM),
        scratch_shapes=scratch + [sem(shape) for shape in sems],
        compiler_params=pltpu.CompilerParams(
            collective_id=0, has_side_effects=True, vmem_limit_bytes=66 * 1000 * 1000
        ),
        name="spectral",
    )(embed, start, wide)


def solution(mesh):
    return jax.shard_map(
        functools.partial(on_device, mesh.shape["rows"], mesh.shape["rep"]),
        mesh=mesh,
        in_specs=(P("rows", None), P("rows", None), P("rows", None)),
        out_specs=P("rows", None),
        check_vma=False,
    )
```

time: 371 us -> 107 us (0.29)
  waiting for transfers between devices: 250 us -> 0 us
  Pallas kernels: 0 us -> 104 us
  other arithmetic: 52.4 us -> 0 us
  starting transfers between devices: 29.4 us -> 0 us
  between operations: 13.5 us -> 0.01 us
  matrix products: 12.4 us -> 0 us
  blocking collectives: 5.65 us -> 0 us
    psum x4 -> x0, waiting for transfers between devices: 201 us -> none  [the longest x2 140 us: on_device(): gram_matrix = lax.psum(jnp.dot(result.T, result, precision=highest), 'rows')]
    pallas_call x0 -> x1, Pallas kernels: none -> 104 us  [on_device(): pl.pallas_call(functools.partial(kernel, n, reps), out_shape=jax.ShapeDty...]
    all_to_all x7 -> x0, waiting for transfers between devices: 49.3 us -> none  [the longest x2 13.7 us: on_device(): lax.all_to_all(reverse, 'rows', split_axis=0, concat_axis=0, tiled=True)]
    another operation x10 -> x0, other arithmetic: 45.7 us -> none  [the longest x6 24.8 us: orthonormal(): lower_factor = jnp.linalg.cholesky(gram_matrix)]
    all_to_all x7 -> x0, starting transfers between devices: 29.1 us -> none  [the longest x2 7.89 us: on_device(): lax.all_to_all(outgoing_iterate, 'rows', split_axis=0, concat_axis=0, til...]
    dot_general x13 -> x0, matrix products: 11.4 us -> none  [the longest x2 4.97 us: on_device(): gram_matrix = lax.psum(jnp.dot(result.T, result, precision=highest), 'rows')]
    psum x1 -> x0, blocking collectives: 5.65 us -> none  [on_device(): lax.psum(own_sums + widen(placed_sums, rep_count, quarter_index), 'rep')]
  transfers between devices with their start and end apart: 11 -> 0, of which waited for: 11 -> 0; matrix products, arithmetic and copies ran while one was open for 1% -> 0% of each run, Pallas kernels for 0% -> 0%
where the time goes in v1:
time: 107 us
  Pallas kernels  104 us (97%)
  local copies, waits for them, and re-layouts  2.92 us (3%)
    pallas_call x1, Pallas kernels, on_device(): pl.pallas_call(functools.partial(kernel, n, reps), out_shape=jax.ShapeDty...  104 us

profile of v1, /device:TPU:0, one launch (start us, length us, event | category | flops | bytes accessed | tf_op | source)
XLA Modules:
  0.0 106.8 jit_solution(14680497185347115988)
XLA Ops:
  0.0 0.7 pad_bitcast_fusion
  0.7 0.6 broadcast_in_dim.8.links
  1.3 103.9 %spectral.1 = f32[512,128]{1,0:T(8,128)} custom-call(bf16[512,1024]{1,0:T(8,128)(2,1)} %embed.1, bf16[512,128]{1,0:T(8,128)(2,1)} %start.1, s32[8,128]{1,0:T(8,128)} %broadcast_in_dim.8.links), custom_call_target="tpu_custom_call" | custom-call | tf_op jit(solution)/shard_map/spectral/pallas_call | solution.py:480
  105.2 1.7 %copy.5 = f32[512,128]{1,0:T(8,128)} copy(f32[512,128]{1,0:T(8,128)} %spectral.1) | data formatting | bytes 524288

commit v2 on v1

--- a/solution.py
+++ b/solution.py
@@ -12,6 +12,7 @@
 BLOCKS_DEV = 4
 ITERS = 2
 LANES = 128
+PANEL = 16
 EPSILON = 1e-06
 HIGHEST = lax.Precision.HIGHEST
 F32 = jnp.float32
@@ -33,15 +34,57 @@
     return jnp.broadcast_to(column, (column.shape[0], LANES)).T[0:1, :]
 
 
+def inverse_factor(matrix, inverse):
+    size = matrix.shape[-1]
+    count = size // PANEL
+    per = matrix.shape[1] // PANEL
+    sub = lax.broadcasted_iota(jnp.int32, (PANEL, size), 0)
+    lane = lax.broadcasted_iota(jnp.int32, (PANEL, size), 1)
+    left = [
+        matrix[p // per, (p % per) * PANEL:(p % per + 1) * PANEL, :] for p in range(count)
+    ]
+    right = [jnp.where(lane == sub + p * PANEL, 1.0, 0.0) for p in range(count)]
+    for p in range(count):
+        low = p * PANEL
+        columns = [
+            jnp.broadcast_to(left[p][:, low + j:low + j + 1], (PANEL, size))
+            for j in range(PANEL)
+        ]
+        rows, tracked = left[p], right[p]
+        result = jnp.zeros((PANEL, size), F32)
+        for k in range(PANEL):
+            here = sub == k
+            column = columns[k]
+            pivot = jnp.broadcast_to(column[k:k + 1, :], (PANEL, size))
+            result = jnp.where(here, tracked * lax.rsqrt(pivot), result)
+            scale = 1.0 / pivot
+
+            def cleared(values):
+                row = values[k:k + 1, :] * scale
+                return jnp.where(here, row, values - column * row)
+
+            rows, tracked = cleared(rows), cleared(tracked)
+            for j in range(k + 1, PANEL):
+                columns[j] = cleared(columns[j])
+        for below in range(p + 1, count):
+            base = left[below]
+            for j in range(PANEL):
+                column = base[:, low + j:low + j + 1]
+                right[below] = right[below] - column * tracked[j:j + 1, :]
+                left[below] = left[below] - column * rows[j:j + 1, :]
+        inverse[low:low + PANEL, :] = result
+
+
 def kernel(
     n, reps,
-    embed, start, links, out,
-    link_in, asked, alive, own, picks, pieces, tiles, tiles_t, square,
+    embed_hbm, start_hbm, links, out,
+    embed, start, link_out, link_in, asked, alive, own, picks, pieces, tiles, tiles_t, square,
     u_full, u_out, u_in, rev_out, rev_in, part_out, part_in, y_own, y_in, inv, placed,
     g_out, g_in, slice_out, slice_in, total_out, gram, elim,
+    back_out, back_in, back_sum, degree_out, degree_in,
     link_send, link_recv, embed_send, embed_recv, u_send, u_recv, rev_send, rev_recv,
     part_send, part_recv, y_send, y_recv, g_send, g_recv, slice_send, slice_recv,
-    total_send, total_recv,
+    total_send, total_recv, load_sem, degree_send, degree_recv,
 ):
     me = lax.axis_index("rows")
     quarter = lax.axis_index("rep")
@@ -86,6 +129,12 @@
     def own_at(block, which):
         return pl.ds(pl.multiple_of(block * BLOCK + which * piece, piece), piece)
 
+    load_embed = pltpu.make_async_copy(embed_hbm, embed, load_sem.at[0])
+    load_start = pltpu.make_async_copy(start_hbm, start, load_sem.at[1])
+    load_embed.start()
+    load_start.start()
+    link_out[...] = jnp.full((8, LANES), -1, jnp.int32)
+    link_out[0:1, 0:n] = links[...]
     barrier = pltpu.get_barrier_semaphore()
 
     def greet(distance):
@@ -103,16 +152,17 @@
     pl.semaphore_wait(barrier, n + reps - 2)
 
     def link_copy(s):
-        return to_rows(links, link_in.at[me], link_send.at[s], link_recv.at[me], s)
+        return to_rows(link_out, link_in.at[me], link_send.at[s], link_recv.at[me], s)
 
     def link_got(s):
-        return to_rows(links, link_in.at[s], link_send.at[s], link_recv.at[s], s)
+        return to_rows(link_out, link_in.at[s], link_send.at[s], link_recv.at[s], s)
 
     over(n, lambda d: link_copy(peer(d)).start(), 1)
     lane = lax.broadcasted_iota(jnp.int32, (8, LANES), 1)
-    link_in[me] = links[...]
     pieces[me] = jnp.zeros((piece, features), BF16)
 
+    load_embed.wait()
+    load_start.wait()
     for b in range(blocks):
         own[b] = embed[own_at(b, quarter), :]
     own_flat = own[...].reshape(own_rows, features)
@@ -123,7 +173,7 @@
     scale_row = as_row(slab_scale)
 
     def alive_of(s):
-        entry = jnp.sum(jnp.where(lane == s, links[...], 0).astype(F32), axis=1, keepdims=True)
+        entry = jnp.sum(jnp.where(lane == s, link_out[...], 0).astype(F32), axis=1, keepdims=True)
         alive[s] = jnp.broadcast_to(
             jnp.where(entry[0:1] >= 0.0, 1.0, 0.0), (piece, LANES)
         )
@@ -172,26 +222,22 @@
     over(n // group, tile_chunk)
 
     def product(phase, u_turn):
-        if u_turn is not None:
+        own_us = [u_full[own_at(b, quarter), :] for b in range(blocks)]
+
+        def send_u(d):
+            s = peer(d)
+            chosen = jnp.maximum(asked[s][0:1, :], 0.0)
+            mixed = jnp.zeros((piece, comps), F32)
             for b in range(blocks):
-                own_u = u_full[own_at(b, quarter), :]
-                u_own_parts.append(own_u)
-            own_us = u_own_parts[-blocks:]
-
-            def send_u(d):
-                s = peer(d)
-                chosen = jnp.maximum(asked[s][0:1, :], 0.0)
-                mixed = jnp.zeros((piece, comps), F32)
-                for b in range(blocks):
-                    mixed = mixed + jnp.where(chosen == float(b), 1.0, 0.0) * own_us[b].astype(F32)
-                u_out[u_turn, s] = mixed.astype(BF16)
-                to_rows(
-                    u_out.at[u_turn, s], u_in.at[u_turn, me],
-                    u_send.at[u_turn, s], u_recv.at[u_turn, me], s,
-                ).start()
-
-            over(n, send_u, 1)
-            u_in[u_turn, me] = jnp.zeros((piece, comps), BF16)
+                mixed = mixed + jnp.where(chosen == float(b), 1.0, 0.0) * own_us[b].astype(F32)
+            u_out[u_turn, s] = mixed.astype(BF16)
+            to_rows(
+                u_out.at[u_turn, s], u_in.at[u_turn, me],
+                u_send.at[u_turn, s], u_recv.at[u_turn, me], s,
+            ).start()
+
+        over(n, send_u, 1)
+        u_in[u_turn, me] = jnp.zeros((piece, comps), BF16)
 
         def reverse(index):
             result = dot(tiles[index], u_full[...], ((1,), (0,)))
@@ -207,26 +253,20 @@
             ).start()
 
         over(n, send_rev, 1)
-        if u_turn is None:
-            u_mine = jnp.ones((own_rows, comps), BF16)
-        else:
-            u_mine = jnp.concatenate(own_us, axis=0)
+        u_mine = jnp.concatenate(own_us, axis=0)
         forward = dot(square[...], u_mine, ((1,), (0,)))
-        if u_turn is not None:
-            def u_got(d):
-                s = peer(d)
-                to_rows(
-                    u_out.at[u_turn, s], u_in.at[u_turn, s],
-                    u_send.at[u_turn, s], u_recv.at[u_turn, s], s,
-                ).wait_recv()
-
-            over(n, u_got, 1)
+
+        def u_got(d):
+            s = peer(d)
+            to_rows(
+                u_out.at[u_turn, s], u_in.at[u_turn, s],
+                u_send.at[u_turn, s], u_recv.at[u_turn, s], s,
+            ).wait_recv()
+
+        over(n, u_got, 1)
 
         def forward_chunk(index, sofar):
-            if u_turn is None:
-                fetched = jnp.ones((chunk, comps), BF16)
-            else:
-                fetched = u_in[u_turn, pl.ds(index * group, group)].reshape(chunk, comps)
+            fetched = u_in[u_turn, pl.ds(index * group, group)].reshape(chunk, comps)
             return sofar + dot(tiles_t[index], fetched, ((1,), (0,)))
 
         if n // group == 1:
@@ -286,24 +326,63 @@
                 y_send.at[phase, t], y_recv.at[phase, t], t,
             ).wait_recv()
 
-    u_own_parts = []
-    u_full[...] = jnp.ones((slab, comps), BF16)
-    degree = product(0, None)
-    share(0, degree)
-    inv_own = lax.rsqrt(degree)
-    shared(0)
-    for t in range(reps):
+    def back_chunk(index):
+        sums = dot(jnp.ones((8, slab), BF16), tiles_t[index], ((1,), (0,)))
+        for g in range(group):
+            back_out[index * group + g, :, 0:piece] = sums[:, g * piece:(g + 1) * piece]
+
+    def send_back(d):
+        s = peer(d)
+        to_rows(back_out.at[s], back_in.at[me], rev_send.at[0, s], rev_recv.at[0, me], s).start()
+
+    def back_got(d):
+        s = peer(d)
+        to_rows(
+            back_out.at[s], back_in.at[s], rev_send.at[0, s], rev_recv.at[0, s], s
+        ).wait_recv()
+        value = back_in[s]
         for b in range(blocks):
-            low = b * BLOCK + t * piece
-            inv[low:low + piece] = lax.rsqrt(y_in[0, t, b * piece:(b + 1) * piece])
+            back_sum[b] = back_sum[b] + jnp.where(asked[s] == float(b), 1.0, 0.0) * value
+
+    back_out[...] = jnp.zeros_like(back_out)
+    over(n // group, back_chunk)
+    over(n, send_back, 1)
+    back_sum[...] = jnp.zeros_like(back_sum)
+    degree_out[...] = dot(jnp.ones((8, own_rows), BF16), square[...], ((1,), (1,)))
+
+    def own_chunk(index):
+        degree_out[...] = degree_out[...] + dot(
+            jnp.ones((8, chunk), BF16), tiles[index], ((1,), (0,))
+        )
+
+    over(n // group, own_chunk)
+    over(n, back_got, 1)
+    for b in range(blocks):
+        at = pl.ds(b * BLOCK, BLOCK)
+        degree_out[:, at] = degree_out[:, at] + pltpu.roll(back_sum[b], quarter * piece, 1)
+
+    def degree_copy(t):
+        return to_rep(
+            degree_out, degree_in.at[quarter], degree_send.at[t], degree_recv.at[quarter], t
+        )
+
+    for d in range(1, reps):
+        degree_copy(rep_peer(d)).start()
+    degree_in[quarter] = degree_out[...]
+    for d in range(1, reps):
+        t = rep_peer(d)
+        to_rep(
+            degree_out, degree_in.at[t], degree_send.at[t], degree_recv.at[t], t
+        ).wait_recv()
+    inv_row = lax.rsqrt(jnp.sum(degree_in[...], axis=0))[0:1]
+    for b in range(blocks):
+        inv[b * BLOCK:(b + 1) * BLOCK] = jnp.broadcast_to(
+            inv_row[:, b * BLOCK:(b + 1) * BLOCK], (LANES, BLOCK)
+        ).T
+    inv_own = jnp.concatenate([inv[own_at(b, quarter), 0:comps] for b in range(blocks)], axis=0)
     u_full[...] = (start[...].astype(F32) * inv[...]).astype(BF16)
 
     part = comps // reps
-    sub_c = lax.broadcasted_iota(jnp.int32, (comps, comps), 0)
-    lane_c = lax.broadcasted_iota(jnp.int32, (comps, comps), 1)
-    sub_1 = lax.broadcasted_iota(jnp.int32, (comps, 1), 0)
-    lane_1 = lax.broadcasted_iota(jnp.int32, (1, comps), 1)
-
     for turn in range(ITERS):
         phase = turn + 1
         y_mine = product(phase, turn) * inv_own
@@ -359,23 +438,8 @@
                 total_send.at[turn, t], total_recv.at[turn, t], t,
             ).wait_recv()
 
-        elim[:, 0:comps] = gram[turn].reshape(comps, comps)
-        elim[:, comps:2 * comps] = jnp.where(sub_c == lane_c, 1.0, 0.0)
-
-        def eliminate(k, carry):
-            row = elim[pl.ds(k, 1), :]
-            left = elim[:, 0:comps]
-            column = jnp.sum(jnp.where(lane_c == k, left, 0.0), axis=1, keepdims=True)
-            pivot = jnp.sum(jnp.where(lane_1 == k, row[:, 0:comps], 0.0), axis=1, keepdims=True)
-            factor = jnp.where(sub_1 > k, column / pivot, 0.0)
-            elim[...] = elim[...] - factor * row
-            return carry
-
-        lax.fori_loop(0, comps, eliminate, 0)
-        pivots = jnp.sum(
-            jnp.where(sub_c == lane_c, elim[:, 0:comps], 0.0), axis=1, keepdims=True
-        )
-        lower_inv = elim[:, comps:2 * comps] * lax.rsqrt(pivots)
+        inverse_factor(gram.at[turn], elim)
+        lower_inv = elim[...]
         shared(phase)
         last = turn == ITERS - 1
         for t in range(reps):
@@ -392,7 +456,8 @@
         s = peer(d)
         link_copy(s).wait_send()
         to_rows(picks.at[s], pieces.at[me], embed_send.at[s], embed_recv.at[me], s).wait_send()
-        for phase in range(ITERS + 1):
+        to_rows(back_out.at[s], back_in.at[me], rev_send.at[0, s], rev_recv.at[0, me], s).wait_send()
+        for phase in range(1, ITERS + 1):
             to_rows(
                 rev_out.at[phase, s], rev_in.at[phase, me],
                 rev_send.at[phase, s], rev_recv.at[phase, me], s,
@@ -410,7 +475,8 @@
     over(n, sent_rows, 1)
     for d in range(1, reps):
         t = rep_peer(d)
-        for phase in range(ITERS + 1):
+        degree_copy(t).wait_send()
+        for phase in range(1, ITERS + 1):
             to_rep(
                 part_out.at[phase, t], part_in.at[phase, quarter],
                 part_send.at[phase, t], part_recv.at[phase, quarter], t,
@@ -438,12 +504,12 @@
     part = comps // reps
     group = min(n, 8)
     phases = ITERS + 1
-    wide = jnp.broadcast_to(
-        jnp.pad(links, ((0, 0), (0, LANES - n)), constant_values=-1), (8, LANES)
-    )
     vmem = pltpu.VMEM
     sem = pltpu.SemaphoreType.DMA
     scratch = [
+        vmem((slab, features), BF16),
+        vmem((slab, comps), BF16),
+        vmem((8, LANES), jnp.int32),
         vmem((n, 8, LANES), jnp.int32),
         vmem((n, 8, LANES), F32),
         vmem((n, piece, LANES), F32),
@@ -470,24 +536,30 @@
         vmem((ITERS, n, part, comps), F32),
         vmem((ITERS, part, comps), F32),
         vmem((ITERS, reps, part, comps), F32),
-        vmem((comps, 2 * comps), F32),
+        vmem((comps, comps), F32),
+        vmem((n, 8, LANES), F32),
+        vmem((n, 8, LANES), F32),
+        vmem((BLOCKS_DEV, 8, LANES), F32),
+        vmem((8, slab), F32),
+        vmem((reps, 8, slab), F32),
     ]
     sems = [
         (n,), (n,), (n,), (n,), (ITERS, n), (ITERS, n), (phases, n), (phases, n),
         (phases, reps), (phases, reps), (phases, reps), (phases, reps),
         (ITERS, reps), (ITERS, reps), (ITERS, n), (ITERS, n), (ITERS, reps), (ITERS, reps),
+        (2,), (reps,), (reps,),
     ]
     return pl.pallas_call(
         functools.partial(kernel, n, reps),
         out_shape=jax.ShapeDtypeStruct((slab, comps), F32),
-        in_specs=[pl.BlockSpec(memory_space=pltpu.VMEM)] * 3,
+        in_specs=[pl.BlockSpec(memory_space=pl.ANY)] * 2 + [pl.BlockSpec(memory_space=pltpu.VMEM)],
         out_specs=pl.BlockSpec(memory_space=pltpu.VMEM),
         scratch_shapes=scratch + [sem(shape) for shape in sems],
         compiler_params=pltpu.CompilerParams(
             collective_id=0, has_side_effects=True, vmem_limit_bytes=66 * 1000 * 1000
         ),
         name="spectral",
-    )(embed, start, wide)
+    )(embed, start, links)
 
 
 def solution(mesh):

time: 107 us -> 81.5 us (0.76)
  Pallas kernels: 104 us -> 79.6 us
  local copies, waits for them, and re-layouts: 2.92 us -> 1.67 us
    pallas_call x1, Pallas kernels: 104 us -> 79.6 us  [on_device(): pl.pallas_call(functools.partial(kernel, n, reps), out_shape=jax.ShapeDty...]
    broadcast_in_dim x2 -> x0, local copies, waits for them, and re-layouts: 1.25 us -> none  [on_device(): jnp.broadcast_to(jnp.pad(links, ((0, 0), (0, LANES - n)), constant_values...]
where the time goes in v2:
time: 81.5 us; the launch traced here: 81.3 us
  Pallas kernels  79.6 us (98%)
  local copies, waits for them, and re-layouts  1.67 us (2%)
    pallas_call x1, Pallas kernels, on_device(): pl.pallas_call(functools.partial(kernel, n, reps), out_shape=jax.ShapeDty...  79.6 us
    unnamed x1, local copies, waits for them, and re-layouts  1.67 us

profile of v2, /device:TPU:0, one launch (start us, length us, event | category | flops | bytes accessed | tf_op | source)
XLA Modules:
  0.0 81.3 jit_solution(18037365595709384005)
XLA Ops:
  0.0 79.6 %spectral.1 = f32[512,128]{1,0:T(8,128)} custom-call(bf16[512,1024]{1,0:T(8,128)(2,1)} %embed_hbm.1, bf16[512,128]{1,0:T(8,128)(2,1)} %start_hbm.1, s32[1,8]{1,0:T(1,128)} %links.1), custom_call_target="tpu_custom_call" | custom-call | tf_op jit(solution)/shard_map/spectral/pallas_call | solution.py:552
  79.6 1.7 %copy.5 = f32[512,128]{1,0:T(8,128)} copy(f32[512,128]{1,0:T(8,128)} %spectral.1) | data formatting | bytes 524288

commit v3 on v2

--- a/solution.py
+++ b/solution.py
@@ -94,7 +94,7 @@
     piece = BLOCK // reps
     own_rows = blocks * piece
     spread = 2.0 / math.sqrt(features)
-    group = min(n, 8)
+    group = max(1, min(n, LANES // piece))
     chunk = group * piece
     unroll = n <= 8
 
@@ -151,15 +151,15 @@
         )
     pl.semaphore_wait(barrier, n + reps - 2)
 
-    def link_copy(s):
-        return to_rows(link_out, link_in.at[me], link_send.at[s], link_recv.at[me], s)
-
-    def link_got(s):
-        return to_rows(link_out, link_in.at[s], link_send.at[s], link_recv.at[s], s)
-
-    over(n, lambda d: link_copy(peer(d)).start(), 1)
+    def link_copy(d):
+        return to_rows(link_out, link_in.at[n - d], link_send.at[d], link_recv.at[n - d], peer(d))
+
+    def link_got(d):
+        return to_rows(link_out, link_in.at[d], link_send.at[d], link_recv.at[d], peer(d))
+
+    over(n, lambda d: link_copy(d).start(), 1)
     lane = lax.broadcasted_iota(jnp.int32, (8, LANES), 1)
-    pieces[me] = jnp.zeros((piece, features), BF16)
+    pieces[0] = jnp.zeros((piece, features), BF16)
 
     load_embed.wait()
     load_start.wait()
@@ -172,9 +172,9 @@
     )
     scale_row = as_row(slab_scale)
 
-    def alive_of(s):
-        entry = jnp.sum(jnp.where(lane == s, link_out[...], 0).astype(F32), axis=1, keepdims=True)
-        alive[s] = jnp.broadcast_to(
+    def alive_of(d):
+        entry = jnp.sum(jnp.where(lane == peer(d), link_out[...], 0).astype(F32), axis=1, keepdims=True)
+        alive[d] = jnp.broadcast_to(
             jnp.where(entry[0:1] >= 0.0, 1.0, 0.0), (piece, LANES)
         )
 
@@ -182,17 +182,17 @@
 
     def pick(d):
         s = peer(d)
-        link_got(s).wait_recv()
+        link_got(d).wait_recv()
         entry = jnp.sum(
-            jnp.where(lane == me, link_in[s], 0).astype(F32), axis=1, keepdims=True
-        )
-        asked[s] = jnp.broadcast_to(entry, (8, LANES))
+            jnp.where(lane == me, link_in[d], 0).astype(F32), axis=1, keepdims=True
+        )
+        asked[d] = jnp.broadcast_to(entry, (8, LANES))
         chosen = jnp.maximum(entry[0:1], 0.0)
         mixed = jnp.zeros((piece, features), F32)
         for b in range(blocks):
             mixed = mixed + jnp.where(chosen == float(b), 1.0, 0.0) * own[b].astype(F32)
-        picks[s] = mixed.astype(BF16)
-        to_rows(picks.at[s], pieces.at[me], embed_send.at[s], embed_recv.at[me], s).start()
+        picks[d] = mixed.astype(BF16)
+        to_rows(picks.at[d], pieces.at[n - d], embed_send.at[d], embed_recv.at[n - d], s).start()
 
     over(n, pick, 1)
 
@@ -205,12 +205,16 @@
 
     def embed_got(d):
         s = peer(d)
-        to_rows(picks.at[s], pieces.at[s], embed_send.at[s], embed_recv.at[s], s).wait_recv()
-
-    over(n, embed_got, 1)
-
-    def tile_chunk(index):
+        to_rows(picks.at[d], pieces.at[d], embed_send.at[d], embed_recv.at[d], s).wait_recv()
+
+
+    def tile_chunk(turned):
+        index = n // group - 1 - turned
         first = index * group
+        if unroll:
+            for g in range(group - 1, -1, -1):
+                if first + g:
+                    embed_got(first + g)
         rows = pieces[pl.ds(first, group)].reshape(chunk, features)
         live = alive[pl.ds(first, group)].reshape(chunk, LANES)[:, 0:1]
         values = dot(rows, embed[...], ((1,), (1,)))
@@ -219,6 +223,8 @@
         tiles[index] = values
         tiles_t[index] = values.astype(F32).T.astype(BF16)
 
+    if not unroll:
+        over(n, embed_got, 1)
     over(n // group, tile_chunk)
 
     def product(phase, u_turn):
@@ -226,18 +232,18 @@
 
         def send_u(d):
             s = peer(d)
-            chosen = jnp.maximum(asked[s][0:1, :], 0.0)
+            chosen = jnp.maximum(asked[d][0:1, :], 0.0)
             mixed = jnp.zeros((piece, comps), F32)
             for b in range(blocks):
                 mixed = mixed + jnp.where(chosen == float(b), 1.0, 0.0) * own_us[b].astype(F32)
-            u_out[u_turn, s] = mixed.astype(BF16)
-            to_rows(
-                u_out.at[u_turn, s], u_in.at[u_turn, me],
-                u_send.at[u_turn, s], u_recv.at[u_turn, me], s,
+            u_out[u_turn, d] = mixed.astype(BF16)
+            to_rows(
+                u_out.at[u_turn, d], u_in.at[u_turn, n - d],
+                u_send.at[u_turn, d], u_recv.at[u_turn, n - d], s,
             ).start()
 
         over(n, send_u, 1)
-        u_in[u_turn, me] = jnp.zeros((piece, comps), BF16)
+        u_in[u_turn, 0] = jnp.zeros((piece, comps), BF16)
 
         def reverse(index):
             result = dot(tiles[index], u_full[...], ((1,), (0,)))
@@ -248,8 +254,8 @@
         def send_rev(d):
             s = peer(d)
             to_rows(
-                rev_out.at[phase, s], rev_in.at[phase, me],
-                rev_send.at[phase, s], rev_recv.at[phase, me], s,
+                rev_out.at[phase, d], rev_in.at[phase, n - d],
+                rev_send.at[phase, d], rev_recv.at[phase, n - d], s,
             ).start()
 
         over(n, send_rev, 1)
@@ -259,8 +265,8 @@
         def u_got(d):
             s = peer(d)
             to_rows(
-                u_out.at[u_turn, s], u_in.at[u_turn, s],
-                u_send.at[u_turn, s], u_recv.at[u_turn, s], s,
+                u_out.at[u_turn, d], u_in.at[u_turn, d],
+                u_send.at[u_turn, d], u_recv.at[u_turn, d], s,
             ).wait_recv()
 
         over(n, u_got, 1)
@@ -269,8 +275,9 @@
             fetched = u_in[u_turn, pl.ds(index * group, group)].reshape(chunk, comps)
             return sofar + dot(tiles_t[index], fetched, ((1,), (0,)))
 
-        if n // group == 1:
-            forward = forward_chunk(0, forward)
+        if unroll:
+            for index in range(n // group):
+                forward = forward_chunk(index, forward)
         else:
             forward = lax.fori_loop(0, n // group, forward_chunk, forward)
         for t in range(reps):
@@ -288,11 +295,11 @@
         def place(d):
             s = peer(d)
             to_rows(
-                rev_out.at[phase, s], rev_in.at[phase, s],
-                rev_send.at[phase, s], rev_recv.at[phase, s], s,
-            ).wait_recv()
-            chosen = asked[s][0:1, :]
-            value = rev_in[phase, s]
+                rev_out.at[phase, d], rev_in.at[phase, d],
+                rev_send.at[phase, d], rev_recv.at[phase, d], s,
+            ).wait_recv()
+            chosen = asked[d][0:1, :]
+            value = rev_in[phase, d]
             for b in range(blocks):
                 at = pl.ds(b * piece, piece)
                 placed[at, :] = placed[at, :] + jnp.where(chosen == float(b), 1.0, 0.0) * value
@@ -333,16 +340,16 @@
 
     def send_back(d):
         s = peer(d)
-        to_rows(back_out.at[s], back_in.at[me], rev_send.at[0, s], rev_recv.at[0, me], s).start()
+        to_rows(back_out.at[d], back_in.at[n - d], rev_send.at[0, d], rev_recv.at[0, n - d], s).start()
 
     def back_got(d):
         s = peer(d)
         to_rows(
-            back_out.at[s], back_in.at[s], rev_send.at[0, s], rev_recv.at[0, s], s
+            back_out.at[d], back_in.at[d], rev_send.at[0, d], rev_recv.at[0, d], s
         ).wait_recv()
-        value = back_in[s]
+        value = back_in[d]
         for b in range(blocks):
-            back_sum[b] = back_sum[b] + jnp.where(asked[s] == float(b), 1.0, 0.0) * value
+            back_sum[b] = back_sum[b] + jnp.where(asked[d] == float(b), 1.0, 0.0) * value
 
     back_out[...] = jnp.zeros_like(back_out)
     over(n // group, back_chunk)
@@ -410,14 +417,14 @@
             s = peer(d)
             to_rows(
                 slice_out.at[turn], slice_in.at[turn, me],
-                slice_send.at[turn, s], slice_recv.at[turn, me], s,
+                slice_send.at[turn, d], slice_recv.at[turn, n - d], s,
             ).start()
 
         def slice_got(d):
             s = peer(d)
             to_rows(
                 slice_out.at[turn], slice_in.at[turn, s],
-                slice_send.at[turn, s], slice_recv.at[turn, s], s,
+                slice_send.at[turn, d], slice_recv.at[turn, d], s,
             ).wait_recv()
 
         over(n, send_slice, 1)
@@ -454,22 +461,22 @@
 
     def sent_rows(d):
         s = peer(d)
-        link_copy(s).wait_send()
-        to_rows(picks.at[s], pieces.at[me], embed_send.at[s], embed_recv.at[me], s).wait_send()
-        to_rows(back_out.at[s], back_in.at[me], rev_send.at[0, s], rev_recv.at[0, me], s).wait_send()
+        link_copy(d).wait_send()
+        to_rows(picks.at[d], pieces.at[n - d], embed_send.at[d], embed_recv.at[n - d], s).wait_send()
+        to_rows(back_out.at[d], back_in.at[n - d], rev_send.at[0, d], rev_recv.at[0, n - d], s).wait_send()
         for phase in range(1, ITERS + 1):
             to_rows(
-                rev_out.at[phase, s], rev_in.at[phase, me],
-                rev_send.at[phase, s], rev_recv.at[phase, me], s,
+                rev_out.at[phase, d], rev_in.at[phase, n - d],
+                rev_send.at[phase, d], rev_recv.at[phase, n - d], s,
             ).wait_send()
         for turn in range(ITERS):
             to_rows(
-                u_out.at[turn, s], u_in.at[turn, me],
-                u_send.at[turn, s], u_recv.at[turn, me], s,
+                u_out.at[turn, d], u_in.at[turn, n - d],
+                u_send.at[turn, d], u_recv.at[turn, n - d], s,
             ).wait_send()
             to_rows(
                 slice_out.at[turn], slice_in.at[turn, me],
-                slice_send.at[turn, s], slice_recv.at[turn, me], s,
+                slice_send.at[turn, d], slice_recv.at[turn, n - d], s,
             ).wait_send()
 
     over(n, sent_rows, 1)
@@ -502,7 +509,7 @@
     piece = BLOCK // reps
     own_rows = BLOCKS_DEV * piece
     part = comps // reps
-    group = min(n, 8)
+    group = max(1, min(n, LANES // piece))
     phases = ITERS + 1
     vmem = pltpu.VMEM
     sem = pltpu.SemaphoreType.DMA

time: 81.5 us -> 82 us (level)
  no operation moved by 1% of the time
where the time goes in v3:
time: 82 us; the launch traced here: 81.8 us
  Pallas kernels  80.1 us (98%)
  local copies, waits for them, and re-layouts  1.67 us (2%)
    pallas_call x1, Pallas kernels, on_device(): pl.pallas_call(functools.partial(kernel, n, reps), out_shape=jax.ShapeDty...  80.1 us
    unnamed x1, local copies, waits for them, and re-layouts  1.67 us

profile of v3, /device:TPU:0, one launch (start us, length us, event | category | flops | bytes accessed | tf_op | source)
XLA Modules:
  0.0 81.8 jit_solution(15870812338741776855)
XLA Ops:
  0.0 80.1 %spectral.1 = f32[512,128]{1,0:T(8,128)} custom-call(bf16[512,1024]{1,0:T(8,128)(2,1)} %embed_hbm.1, bf16[512,128]{1,0:T(8,128)(2,1)} %start_hbm.1, s32[1,8]{1,0:T(1,128)} %links.1), custom_call_target="tpu_custom_call" | custom-call | tf_op jit(solution)/shard_map/spectral/pallas_call | solution.py:559
  80.1 1.7 %copy.5 = f32[512,128]{1,0:T(8,128)} copy(f32[512,128]{1,0:T(8,128)} %spectral.1) | data formatting | bytes 524288

commit v4 on v3

--- a/solution.py
+++ b/solution.py
@@ -247,7 +247,7 @@
 
         def reverse(index):
             result = dot(tiles[index], u_full[...], ((1,), (0,)))
-            rev_out[phase, pl.ds(index * group, group)] = result.reshape(group, piece, comps)
+            rev_out[phase, pl.ds(index * group, group)] = result.astype(BF16).reshape(group, piece, comps)
 
         over(n // group, reverse)
 
@@ -299,7 +299,7 @@
                 rev_send.at[phase, d], rev_recv.at[phase, d], s,
             ).wait_recv()
             chosen = asked[d][0:1, :]
-            value = rev_in[phase, d]
+            value = rev_in[phase, d].astype(F32)
             for b in range(blocks):
                 at = pl.ds(b * piece, piece)
                 placed[at, :] = placed[at, :] + jnp.where(chosen == float(b), 1.0, 0.0) * value
@@ -529,8 +529,8 @@
         vmem((slab, comps), BF16),
         vmem((ITERS, n, piece, comps), BF16),
         vmem((ITERS, n, piece, comps), BF16),
-        vmem((phases, n, piece, comps), F32),
-        vmem((phases, n, piece, comps), F32),
+        vmem((phases, n, piece, comps), BF16),
+        vmem((phases, n, piece, comps), BF16),
         vmem((phases, reps, own_rows, comps), F32),
         vmem((phases, reps, own_rows, comps), F32),
         vmem((phases, own_rows, comps), F32),

time: 82 us -> 81.9 us (level)
  no operation moved by 1% of the time
where the time goes in v4:
time: 81.9 us; the launch traced here: 81.7 us
  Pallas kernels  80 us (98%)
  local copies, waits for them, and re-layouts  1.67 us (2%)
    pallas_call x1, Pallas kernels, on_device(): pl.pallas_call(functools.partial(kernel, n, reps), out_shape=jax.ShapeDty...  80 us
    unnamed x1, local copies, waits for them, and re-layouts  1.67 us

profile of v4, /device:TPU:0, one launch (start us, length us, event | category | flops | bytes accessed | tf_op | source)
XLA Modules:
  0.0 81.7 jit_solution(7435822058189744135)
XLA Ops:
  0.0 80.0 %spectral.1 = f32[512,128]{1,0:T(8,128)} custom-call(bf16[512,1024]{1,0:T(8,128)(2,1)} %embed_hbm.1, bf16[512,128]{1,0:T(8,128)(2,1)} %start_hbm.1, s32[1,8]{1,0:T(1,128)} %links.1), custom_call_target="tpu_custom_call" | custom-call | tf_op jit(solution)/shard_map/spectral/pallas_call | solution.py:559
  80.1 1.7 %copy.5 = f32[512,128]{1,0:T(8,128)} copy(f32[512,128]{1,0:T(8,128)} %spectral.1) | data formatting | bytes 524288
